TPU v7x, 128 devices: a whole 4x4x4 slice. The times are simulated.
128 devices in a mesh: group: 4 (over x), bulk: 32 (over z, y, core).
Axes of the slice: x: 4, y: 4, z: 4, core: 2. Of those that a mesh axis runs over, the one named last changes fastest.
Arguments:
- rhs: float32 [512, 64, 128], P(('group', 'bulk')), may hold values from -90 to 90, as said below
- diag_tiles: float32 [512, 128, 128], P(('group', 'bulk')), may hold values from -0.06 to 0.06
- offdiag_blocks: float32 [512, 11, 128, 128], P(('group', 'bulk')), may hold values from -0.026 to 0.026
- coupling: float32 [256, 4, 128, 128], P(('group', 'bulk')), may hold values from -0.05 to 0.05, as said below
- col_index: int32 [512, 11], replicated, may hold values from 0 to 511, as said below
- load: int32 [512], replicated, may hold values from 3 to 11
- new_slot: int32 [512], replicated, may hold values from 0 to 511, as said below
Outputs:
- solution_out: float32 [512, 64, 128], P(('group', 'bulk'))
- residual_out: float32 [512, 64, 128], P(('group', 'bulk'))
Inputs may be any that keep to these rules, and one draw needn't show every extreme that they name: `rhs`: made of random entries times scales of the rows and of the columns. `coupling`: entry [d * 2 + k, h] is the transpose of entry [(h * 32 + d % 32) * 2 + k, d // 32]. `col_index`: for each part g and each tile position t, the column t of the 128 block rows of part g is a permutation of that part's slots g * 128 to (g + 1) * 128 - 1. Of the 44 entries of the 4 block rows of one device (slots d * 4 to (d + 1) * 4 - 1), at most 2 name slots of any one device, and exactly 2 name slots of some device. `new_slot`: A permutation. On every device exactly one block row moves, from a slot k with 2 <= k % 4; it stays in its part, goes from owner b to owner b XOR m, where m (1 to 31) is one number for the whole part, and takes the slot that the moving row of that device leaves.
All inputs are finite; a program needn't handle non-finite values.
Results may differ from a plain program's by a relative error of at most 0.0003.
Values sent between devices are 32-bit elements; how exact they have to be, the bound alone decides.
A program may use at most 64 MiB of HBM per device.

v0:
```python
import jax
import jax.numpy as jnp
from jax import lax
from jax.sharding import PartitionSpec as P

highest = lax.Precision.HIGHEST
diagonal_shift = 4.0


def from_partner(value, axis, bit):
    mask = 2**bit
    pairs = [(source, source ^ mask) for source in range(lax.axis_size(axis))]
    return lax.ppermute(value, axis, pairs)


def chol_apply(matrix, right):
    factor = jnp.linalg.cholesky(matrix)
    middle = lax.linalg.triangular_solve(factor, right, left_side=True, lower=True)
    return lax.linalg.triangular_solve(factor, middle, left_side=True, lower=True, transpose_a=True)


def global_gram(left, right):
    partial_gram = jnp.einsum("snt,smt->nm", left, right, precision=highest)
    total = lax.psum(partial_gram, ("group", "bulk"))
    return 0.5 * (total + total.T)


def operate(vectors, diag, masked, column_ids, coupling):
    row_count = vectors.shape[0]
    boundary_rows = coupling.shape[0]
    part_count = coupling.shape[1]
    group_rows = row_count * lax.axis_size("bulk")
    border = lax.all_gather(vectors[:boundary_rows], "group", axis=0, tiled=True)
    final_output = diagonal_shift * vectors + jnp.einsum(
        "rnj,rij->rni", vectors, diag, precision=highest
    )
    returned = jnp.einsum("rni,rkij->rknj", vectors, masked, precision=highest)
    flat_terms = returned.reshape((-1,) + vectors.shape[1:])
    panel = lax.all_gather(vectors, "bulk", axis=0, tiled=True)
    buffer = jax.ops.segment_sum(flat_terms, column_ids.reshape(-1), num_segments=group_rows)
    owed = lax.psum_scatter(buffer, "bulk", scatter_dimension=0, tiled=True)
    picked = panel[column_ids]
    final_output = (
        final_output + jnp.einsum("rknj,rkij->rni", picked, masked, precision=highest) + owed
    )
    border = border.reshape((part_count, boundary_rows) + vectors.shape[1:])
    crossed = jnp.einsum("khij,hknj->kni", coupling, border, precision=highest)
    return final_output.at[:boundary_rows].add(crossed)


def advance(state, diag, masked, column_ids, coupling, last_step):
    solution, resid, direction, gram_rr = state
    image = operate(direction, diag, masked, column_ids, coupling)
    gram_pq = global_gram(direction, image)
    alpha = chol_apply(gram_pq, gram_rr)
    solution = solution + jnp.einsum("mn,smt->snt", alpha, direction, precision=highest)
    resid = resid - jnp.einsum("mn,smt->snt", alpha, image, precision=highest)
    if not last_step:
        gram_new = global_gram(resid, resid)
        beta = chol_apply(gram_rr, gram_new)
        direction = resid + jnp.einsum("mn,smt->snt", beta, direction, precision=highest)
        gram_rr = gram_new
    return (solution, resid, direction, gram_rr)


def local(rhs, diag_tiles, offdiag_blocks, coupling, col_index, load, new_slot):
    row_count = rhs.shape[0]
    off_count = offdiag_blocks.shape[1]
    bulk_count = lax.axis_size("bulk")
    group_rows = row_count * bulk_count
    my_group = lax.axis_index("group")
    my_bulk = lax.axis_index("bulk")
    first_slot = (my_group * bulk_count + my_bulk) * row_count
    group_base = my_group * group_rows
    own_slots = first_slot + jnp.arange(row_count, dtype=jnp.int32)
    tile_ids = jnp.arange(off_count, dtype=jnp.int32)
    old_columns = col_index[own_slots] - group_base
    old_mask = (tile_ids[None, :] < load[own_slots][:, None]).astype(jnp.float32)
    old_masked = offdiag_blocks * old_mask[:, :, None, None]
    own_new = new_slot[own_slots]
    leaving = jnp.argmax((own_new != own_slots).astype(jnp.int32))
    target = own_new[leaving]
    target_bulk = target // row_count % bulk_count
    xor_mask = jnp.bitwise_xor(target_bulk, my_bulk)
    start_state = (jnp.zeros_like(rhs), rhs, rhs, global_gram(rhs, rhs))
    state = advance(start_state, diag_tiles, old_masked, old_columns, coupling, False)
    solution, resid, direction, gram_rr = state
    pieces = [
        offdiag_blocks[leaving],
        diag_tiles[leaving],
        solution[leaving],
        resid[leaving],
        direction[leaving],
    ]
    flat = jnp.concatenate([piece.reshape(-1) for piece in pieces])
    for bit_pos in range(bulk_count.bit_length() - 1):
        partner = from_partner(flat, "bulk", bit_pos)
        chosen = jnp.bitwise_and(jnp.right_shift(xor_mask, bit_pos), 1) == 1
        flat = jnp.where(chosen, partner, flat)
    outputs = []
    offset = 0
    for piece in pieces:
        outputs.append(flat[offset : offset + piece.size].reshape(piece.shape))
        offset = offset + piece.size
    moved_off = offdiag_blocks.at[leaving].set(outputs[0])
    moved_diag = diag_tiles.at[leaving].set(outputs[1])
    solution = solution.at[leaving].set(outputs[2])
    resid = resid.at[leaving].set(outputs[3])
    direction = direction.at[leaving].set(outputs[4])
    inverse = (
        jnp.zeros_like(new_slot).at[new_slot].set(jnp.arange(new_slot.shape[0], dtype=jnp.int32))
    )
    old_rows = inverse[own_slots]
    new_columns = new_slot[col_index[old_rows]] - group_base
    new_mask = (tile_ids[None, :] < load[old_rows][:, None]).astype(jnp.float32)
    new_masked = moved_off * new_mask[:, :, None, None]
    state = advance(
        (solution, resid, direction, gram_rr), moved_diag, new_masked, new_columns, coupling, True
    )
    return (state[0], state[1])


def solution(mesh):
    return jax.shard_map(
        local,
        mesh=mesh,
        in_specs=(
            P(("group", "bulk"), None, None),
            P(("group", "bulk"), None, None),
            P(("group", "bulk"), None, None, None),
            P(("group", "bulk"), None, None, None),
            P(),
            P(),
            P(),
        ),
        out_specs=(P(("group", "bulk"), None, None), P(("group", "bulk"), None, None)),
        check_vma=False,
    )
```

profile of v0, /device:TPU:1, one launch (start us, length us, event | category | flops | bytes accessed | tf_op | source)
XLA Modules:
  0.0 662.4 jit_solution(1041182074401895514)
XLA Ops:
  7.3 1.9 copy.86
  9.9 1.6 copy.40
  12.1 2.6 scatter_custom_fusion.1
  15.9 1.5 gather_fusion
  18.7 2.2 gather_fusion.5
  25.3 3.2 fusion.4
  28.5 2.5 broadcast.320.clone
  31.0 8.0 %scatter_fusion = f32[128,64,128]{2,1,0:T(8,128)} fusion(f32[128,64,128]{2,1,0:T(8,128)} %broadcast.320.clone, s32[44]{0:T(128)} %reshape.516, f32[44,64,128]{2,1,0:T(8,128)} %bitcast.222), kind=kCustom, calls=%fused_computation.9 | custom fusion | flops 360448 | bytes 4325552 | tf_op jit(solution)/shard_map/scatter-add | solution.py:40
  40.2 1.3 fusion.68
  45.5 13.0 %all_gather.13 = f32[8,64,128]{2,1,0:T(8,128)} all-gather(f32[2,64,128]{2,1,0:T(8,128)} %slice.208), channel_id=1, replica_groups=mesh['group'=4,'bulk'=32] {'group'}, dimensions={0}, use_global_device_ids=true | all-gather | bytes 327680 | tf_op jit(solution)/shard_map/all_gather | solution.py:33
  60.9 1.5 bitcast_dynamic-update-slice_fusion
  62.4 4.0 gather_fusion.1
  66.4 5.4 fusion.12
  71.8 71.6 %reduce-scatter.3.cloned.1.call-done = f32[4,64,128]{2,1,0:T(8,128)} async-done(((f32[128,64,128]{2,1,0:T(8,128)}), f32[4,64,128]{2,1,0:T(8,128)}) %reduce-scatter.3.cloned.1.call-update) | async-done | bytes 131088 | tf_op jit(solution)/shard_map/reduce_scatter | solution.py:41
  143.4 1.7 fusion.21
  145.1 1.6 fusion.29
  148.2 66.3 %all-reduce = (f32[64,64]{1,0:T(8,128)}, f32[64,64]{1,0:T(8,128)}) all-reduce(f32[64,64]{1,0:T(8,128)} %convolution_bitcast_fusion.11, f32[64,64]{1,0:T(8,128)} %convolution_bitcast_fusion.12), channel_id=1, replica_groups=mesh['group'=4,'bulk'=32] {'group','bulk'}, use_global_device_ids=true, to_apply=%region_5.7 | all-reduce | flops 8192 | bytes 65536 | tf_op jit(solution)/shard_map/psum | solution.py:24
  214.6 1.4 copy.45
  216.0 1.4 fusion.56
  217.4 1.4 copy.48
  218.8 1.5 copy.43
  220.3 1.4 fusion.61
  221.7 1.4 copy.44
  223.1 1.4 fusion.60
  224.5 7.2 %cholesky.59 = f32[64,64]{1,0:T(8,128)} custom-call(f32[64,64]{1,0:T(8,128)} %fusion.60), custom_call_target="Cholesky" | custom-call | tf_op jit(solution)/shard_map/jit(cholesky)/cholesky | solution.py:17
  233.2 2.1 fusion.36
  235.3 6.3 custom-call.13
  243.6 1.8 fusion.25
  246.3 1.4 fusion.55
  247.7 7.2 %cholesky.70 = f32[64,64]{1,0:T(8,128)} custom-call(f32[64,64]{1,0:T(8,128)} %fusion.55), custom_call_target="Cholesky" | custom-call | tf_op jit(solution)/shard_map/jit(cholesky)/cholesky | solution.py:17
  256.4 2.1 fusion.37
  258.5 6.3 custom-call.15
  264.7 1.8 convolution_bitcast_fusion.9
  266.6 63.0 %psum.30 = f32[64,64]{1,0:T(8,128)} all-reduce(f32[64,64]{1,0:T(8,128)} %convolution_bitcast_fusion.9), channel_id=1, replica_groups=mesh['group'=4,'bulk'=32] {'group','bulk'}, use_global_device_ids=true, to_apply=%region_8.12 | all-reduce | flops 4096 | bytes 32768 | tf_op jit(solution)/shard_map/psum | solution.py:24
  329.6 1.4 copy.49
  334.2 1.4 bitcast_dynamic-update-slice_fusion.3
  335.6 1.4 bitcast_dynamic-update-slice_fusion.2
  341.3 2.2 broadcast_select_fusion
  344.7 20.3 %collective-permute-done.1 = f32[221184]{0:T(1024)} collective-permute-done((f32[221184]{0:T(1024)}, f32[221184]{0:T(1024)}, u32[]{:S(2)}, u32[]{:S(2)}) %collective-permute-start.1) | collective-permute-done | bytes 884768 | tf_op jit(solution)/shard_map/ppermute | solution.py:13
  365.0 2.2 broadcast_select_fusion.1
  367.2 2.9 collective-permute-start.2
  370.2 19.2 %collective-permute-done.2 = f32[221184]{0:T(1024)} collective-permute-done((f32[221184]{0:T(1024)}, f32[221184]{0:T(1024)}, u32[]{:S(2)}, u32[]{:S(2)}) %collective-permute-start.2) | collective-permute-done | bytes 884768 | tf_op jit(solution)/shard_map/ppermute | solution.py:13
  389.4 2.2 broadcast_select_fusion.2
  392.7 18.7 %collective-permute-done.3 = f32[221184]{0:T(1024)} collective-permute-done((f32[221184]{0:T(1024)}, f32[221184]{0:T(1024)}, u32[]{:S(2)}, u32[]{:S(2)}) %collective-permute-start.3) | collective-permute-done | bytes 884768 | tf_op jit(solution)/shard_map/ppermute | solution.py:13
  411.4 2.2 broadcast_select_fusion.3
  413.6 2.3 collective-permute-start.4
  416.7 17.4 %collective-permute-done.4 = f32[221184]{0:T(1024)} collective-permute-done((f32[221184]{0:T(1024)}, f32[221184]{0:T(1024)}, u32[]{:S(2)}, u32[]{:S(2)}) %collective-permute-start.4) | collective-permute-done | bytes 884768 | tf_op jit(solution)/shard_map/ppermute | solution.py:13
  436.2 2.0 fusion.40
  441.4 1.4 and_reduce_fusion
  445.4 3.2 fusion
  448.6 2.5 broadcast.320
  451.1 7.8 %scatter_fusion.1 = f32[128,64,128]{2,1,0:T(8,128)} fusion(f32[128,64,128]{2,1,0:T(8,128)} %broadcast.320, s32[44]{0:T(128)S(1)} %broadcast_subtract_fusion.1, f32[44,64,128]{2,1,0:T(8,128)} %bitcast.223), kind=kCustom, calls=%fused_computation.11 | custom fusion | flops 360448 | bytes 4325552 | tf_op jit(solution)/shard_map/scatter-add | solution.py:40
  459.2 10.1 %all_gather.15 = f32[8,64,128]{2,1,0:T(8,128)} all-gather(f32[2,64,128]{2,1,0:T(8,128)S(1)} %slice.243), channel_id=1, replica_groups=mesh['group'=4,'bulk'=32] {'group'}, dimensions={0}, use_global_device_ids=true | all-gather | bytes 327680 | tf_op jit(solution)/shard_map/all_gather | solution.py:33
  469.3 2.1 fusion.35
  471.4 15.3 %all-gather.5.cloned.1.call-done = f32[128,64,128]{2,1,0:T(8,128)} async-done(((f32[4,64,128]{2,1,0:T(8,128)}), f32[128,64,128]{2,1,0:T(8,128)}) %all-gather.5.cloned.1.call-update) | async-done | bytes 4194320 | tf_op jit(solution)/shard_map/all_gather | solution.py:39
  486.7 4.0 gather_fusion.7
  490.7 5.4 fusion.15
  496.2 73.8 %reduce-scatter.5.cloned.1.call-done = f32[4,64,128]{2,1,0:T(8,128)} async-done(((f32[128,64,128]{2,1,0:T(8,128)}), f32[4,64,128]{2,1,0:T(8,128)}) %reduce-scatter.5.cloned.1.call-update) | async-done | bytes 131088 | tf_op jit(solution)/shard_map/reduce_scatter | solution.py:41
  570.0 1.7 fusion.19
  571.6 1.6 fusion.27
  573.5 66.0 %psum.31 = f32[64,64]{1,0:T(8,128)S(1)} all-reduce(f32[64,64]{1,0:T(8,128)S(1)} %convolution_bitcast_fusion.7), channel_id=1, replica_groups=mesh['group'=4,'bulk'=32] {'group','bulk'}, use_global_device_ids=true, to_apply=%region_13.17 | all-reduce | flops 4096 | bytes 32768 | tf_op jit(solution)/shard_map/psum | solution.py:24
  639.7 5.8 cholesky.81
  646.9 4.9 custom-call.17
  653.1 1.8 fusion.22
  (102 shorter events, 41.5 us)
Async XLA Ops:
  7.2 137.9 %copy-start = (f32[2,4,128,128]{3,2,1,0:T(8,128)S(1)}, f32[2,4,128,128]{3,2,1,0:T(8,128)}, u32[]{:S(2)}) copy-start(f32[2,4,128,128]{3,2,1,0:T(8,128)} %param.29) | copy-start | bytes 1572868
  7.2 18.1 %copy-start.3 = (f32[4,64,128]{2,1,0:T(8,128)S(1)}, f32[4,64,128]{2,1,0:T(8,128)}, u32[]{:S(2)}) copy-start(f32[4,64,128]{2,1,0:T(8,128)} %param.26) | copy-start | bytes 393220
  7.2 16.2 %copy-start.2 = (s32[512]{0:T(512)S(1)}, s32[512]{0:T(512)}, u32[]{:S(2)}) copy-start(s32[512]{0:T(512)} %param.31) | copy-start | bytes 6148
  7.2 4.3 copy-start.1
  7.2 55.2 %all-gather.3.cloned.1.call-start = ((), (), s32[]{:S(2)}) async-start(), calls=%async_computation.2 | async-start | bytes 4325376 | tf_op jit(solution)/shard_map/all_gather | solution.py:39
  7.3 1.9 copy-start.11
  9.9 133.5 %reduce-scatter.3.cloned.1.call-start = ((), (), s32[]{:S(2)}) async-start(), calls=%async_computation.3 | async-start | bytes 4325376 | tf_op jit(solution)/shard_map/reduce_scatter | solution.py:41
  39.0 447.7 %all-gather.5.cloned.1.call-start = ((), (), s32[]{:S(2)}) async-start(), calls=%async_computation.4 | async-start | bytes 4325376 | tf_op jit(solution)/shard_map/all_gather | solution.py:39
  71.8 266.4 %copy-start.13 = (s32[4]{0:T(128)S(1)}, s32[4]{0:T(128)}, u32[]{:S(2)}) copy-start(s32[4]{0:T(128)} %gather_fusion.3) | copy-start | bytes 52
  146.7 0.7 copy-start.7
  334.2 2.8 copy-start.4
  337.6 3.7 collective-permute-start
  343.5 21.5 %collective-permute-start.1 = (f32[221184]{0:T(1024)}, f32[221184]{0:T(1024)}, u32[]{:S(2)}, u32[]{:S(2)}) collective-permute-start(f32[221184]{0:T(1024)} %broadcast_select_fusion), channel_id=1, source_target_pairs={{0,2},{1,3},{2,0},{3,1},{4,6},{5,7},{6,4},{7,5},{8,10},{9,11},{10,... | collective-permute-start | bytes 2654216 | tf_op jit(solution)/shard_map/ppermute | solution.py:13
  367.2 48.7 %copy-start.14 = (s32[3]{0:T(128)S(1)}, s32[3]{0:T(128)}, u32[]{:S(2)}) copy-start(s32[3]{0:T(128)} %constant.237.clone.1) | copy-start | bytes 40
  367.2 49.5 %copy-start.8 = (f32[64,4,128]{2,0,1:T(8,128)S(1)}, f32[64,4,128]{2,0,1:T(8,128)}, u32[]{:S(2)}) copy-start(f32[64,4,128]{2,0,1:T(8,128)} %fusion.73) | copy-start | bytes 393220
  367.2 22.2 %collective-permute-start.2 = (f32[221184]{0:T(1024)}, f32[221184]{0:T(1024)}, u32[]{:S(2)}, u32[]{:S(2)}) collective-permute-start(f32[221184]{0:T(1024)} %broadcast_select_fusion.1), channel_id=1, source_target_pairs={{0,4},{1,5},{2,6},{3,7},{4,0},{5,1},{6,2},{7,3},{8,12},{9,13},{10,... | collective-permute-start | bytes 2654216 | tf_op jit(solution)/shard_map/ppermute | solution.py:13
  391.6 19.8 %collective-permute-start.3 = (f32[221184]{0:T(1024)}, f32[221184]{0:T(1024)}, u32[]{:S(2)}, u32[]{:S(2)}) collective-permute-start(f32[221184]{0:T(1024)} %broadcast_select_fusion.2), channel_id=1, source_target_pairs={{0,8},{1,9},{2,10},{3,11},{4,12},{5,13},{6,14},{7,15},{8,0},{9,1},... | collective-permute-start | bytes 2654216 | tf_op jit(solution)/shard_map/ppermute | solution.py:13
  392.7 47.8 %copy-start.12 = (s32[4,11,1]{1,0,2:T(4,128)S(1)}, s32[4,11,1]{1,0,2:T(4,128)}, u32[]{:S(2)}) copy-start(s32[4,11,1]{1,0,2:T(4,128)} %get-tuple-element.98) | copy-start | bytes 532
  413.6 20.5 %collective-permute-start.4 = (f32[221184]{0:T(1024)}, f32[221184]{0:T(1024)}, u32[]{:S(2)}, u32[]{:S(2)}) collective-permute-start(f32[221184]{0:T(1024)} %broadcast_select_fusion.3), channel_id=1, source_target_pairs={{0,16},{1,17},{2,18},{3,19},{4,20},{5,21},{6,22},{7,23},{8,24},{9,... | collective-permute-start | bytes 2654216 | tf_op jit(solution)/shard_map/ppermute | solution.py:13
  435.3 0.9 copy-start.6
  438.3 0.7 copy-start.9
  438.9 131.0 %reduce-scatter.5.cloned.1.call-start = ((), (), s32[]{:S(2)}) async-start(), calls=%async_computation.5 | async-start | bytes 4325376 | tf_op jit(solution)/shard_map/reduce_scatter | solution.py:41
  440.5 4.9 copy-start.5
  496.2 158.8 %copy-start.10 = (f32[4,64,128]{2,1,0:T(8,128)S(1)}, f32[4,64,128]{2,1,0:T(8,128)}, u32[]{:S(2)}) copy-start(f32[4,64,128]{2,1,0:T(8,128)} %copy-done.9) | copy-start | bytes 393220
Sparse Core Ops, SparseCore 0:
  10.3 49.7 all-gather.2
  63.7 79.6 reduce-scatter.2
  439.1 47.6 all-gather.4
  490.2 79.7 reduce-scatter.4
where the time goes:
time: 666 us; the launch traced here: 662 us
  waiting for transfers between devices  236 us (35%)
  blocking collectives  218 us (33%)
  other arithmetic  90.6 us (14%)
  local copies, waits for them, and re-layouts  50.3 us (8%)
  matrix products  39.5 us (6%)
  between operations  18.6 us (3%)
  starting transfers between devices  8.54 us (1%)
    psum x3, blocking collectives, global_gram(): total = lax.psum(partial_gram, ('group', 'bulk'))  195 us
    reduce_scatter x2, waiting for transfers between devices, operate(): owed = lax.psum_scatter(buffer, 'bulk', scatter_dimension=0, tiled=True)  145 us
    ppermute x5, waiting for transfers between devices, from_partner(): return lax.ppermute(value, axis, pairs)  75.6 us
    another operation x9, other arithmetic, chol_apply(): factor = jnp.linalg.cholesky(matrix)  23.9 us
    all_gather x2, blocking collectives, operate(): lax.all_gather(vectors[:boundary_rows], 'group', axis=0, tiled=True)  23.1 us
    another operation x6, other arithmetic, chol_apply(): lax.linalg.triangular_solve(factor, middle, left_side=True, lower=True, t...  22.2 us
    scatter-add x2, other arithmetic, operate(): jax.ops.segment_sum(flat_terms, column_ids.reshape(-1), num_segments=grou...  15.8 us
    all_gather x2, waiting for transfers between devices, operate(): panel = lax.all_gather(vectors, 'bulk', axis=0, tiled=True)  15.3 us
  transfers between devices with their start and end apart: 9, of which 7 were waited for; matrix products, arithmetic and copies ran while one was open for 12% of the time, Pallas kernels for 0%

commit v1 on v0

--- a/solution.py
+++ b/solution.py
@@ -21,7 +21,9 @@
 
 def global_gram(left, right):
     partial_gram = jnp.einsum("snt,smt->nm", left, right, precision=highest)
-    total = lax.psum(partial_gram, ("group", "bulk"))
+    total = partial_gram
+    for name in ("group", "bulk"):
+        total = lax.psum(total, name)
     return 0.5 * (total + total.T)
 
 

time: 666 us -> 894 us (1.34)
  blocking collectives: 218 us -> 440 us
    psum x3 -> x6, blocking collectives: 195 us -> 417 us  [global_gram(): total = lax.psum(total, name)]
  transfers between devices with their start and end apart: 9 -> 9, of which waited for: 7 -> 7; matrix products, arithmetic and copies ran while one was open for 12% -> 9% of each run, Pallas kernels for 0% -> 0%
where the time goes in v1:
time: 894 us; the launch traced here: 886 us
  blocking collectives  440 us (49%)
  waiting for transfers between devices  241 us (27%)
  other arithmetic  90.6 us (10%)
  local copies, waits for them, and re-layouts  50.3 us (6%)
  matrix products  38.6 us (4%)
  between operations  18.6 us (2%)
    psum x6, blocking collectives, global_gram(): total = lax.psum(total, name)  417 us
    reduce_scatter x2, waiting for transfers between devices, operate(): owed = lax.psum_scatter(buffer, 'bulk', scatter_dimension=0, tiled=True)  145 us
    ppermute x5, waiting for transfers between devices, from_partner(): return lax.ppermute(value, axis, pairs)  83.1 us
    another operation x9, other arithmetic, chol_apply(): factor = jnp.linalg.cholesky(matrix)  23.9 us
    all_gather x2, blocking collectives, operate(): lax.all_gather(vectors[:boundary_rows], 'group', axis=0, tiled=True)  23.3 us
    another operation x6, other arithmetic, chol_apply(): lax.linalg.triangular_solve(factor, middle, left_side=True, lower=True, t...  22.2 us
  transfers between devices with their start and end apart: 9, of which 7 were waited for; matrix products, arithmetic and copies ran while one was open for 9% of the time, Pallas kernels for 0%

profile of v1, /device:TPU:1, one launch (start us, length us, event | category | flops | bytes accessed | tf_op | source)
XLA Modules:
  0.0 885.9 jit_solution(3039968439865863156)
XLA Ops:
  7.3 1.9 copy.86
  9.9 1.6 copy.40
  12.1 2.6 scatter_custom_fusion.1
  15.9 1.5 gather_fusion
  18.7 2.2 gather_fusion.5
  25.3 3.2 fusion.4
  28.5 2.5 broadcast.320.clone
  31.0 8.0 scatter_fusion
  45.5 13.0 %all_gather.13 = f32[8,64,128]{2,1,0:T(8,128)} all-gather(f32[2,64,128]{2,1,0:T(8,128)} %slice.208), channel_id=1, replica_groups=mesh['group'=4,'bulk'=32] {'group'}, dimensions={0}, use_global_device_ids=true | all-gather | bytes 327680 | tf_op jit(solution)/shard_map/all_gather | solution.py:35
  60.9 1.5 bitcast_dynamic-update-slice_fusion
  62.4 4.0 gather_fusion.1
  66.4 5.4 fusion.12
  71.8 71.6 %reduce-scatter.3.cloned.1.call-done = f32[4,64,128]{2,1,0:T(8,128)} async-done(((f32[128,64,128]{2,1,0:T(8,128)}), f32[4,64,128]{2,1,0:T(8,128)}) %reduce-scatter.3.cloned.1.call-update) | async-done | bytes 131088 | tf_op jit(solution)/shard_map/reduce_scatter | solution.py:43
  143.4 1.7 fusion.21
  145.1 1.6 fusion.29
  148.2 14.8 %all-reduce.1 = (f32[64,64]{1,0:T(8,128)}, f32[64,64]{1,0:T(8,128)}) all-reduce(f32[64,64]{1,0:T(8,128)} %convolution_bitcast_fusion.11, f32[64,64]{1,0:T(8,128)} %convolution_bitcast_fusion.12), channel_id=1, replica_groups=mesh['group'=4,'bulk'=32] {'group'}, use_global_device_ids=true, to_apply=%region_6.8 | all-reduce | flops 8192 | bytes 65536 | tf_op jit(solution)/shard_map/psum | solution.py:26
  163.0 125.0 %all-reduce = (f32[64,64]{1,0:T(8,128)}, f32[64,64]{1,0:T(8,128)}) all-reduce(f32[64,64]{1,0:T(8,128)} %get-tuple-element.93, f32[64,64]{1,0:T(8,128)} %get-tuple-element.94), channel_id=1, replica_groups=mesh['group'=4,'bulk'=32] {'bulk'}, use_global_device_ids=true, to_apply=%region_7.9 | all-reduce | flops 8192 | bytes 65536 | tf_op jit(solution)/shard_map/psum | solution.py:26
  288.0 1.4 copy.45
  289.5 1.4 fusion.56
  290.9 1.4 copy.48
  292.3 1.5 copy.43
  293.8 1.4 fusion.61
  295.1 1.4 copy.44
  296.6 1.4 fusion.60
  298.0 7.2 cholesky.59
  306.7 2.1 fusion.36
  308.7 6.3 custom-call.13
  317.0 1.8 fusion.25
  319.8 1.4 fusion.55
  321.2 7.2 cholesky.70
  329.9 2.1 fusion.37
  331.9 6.3 custom-call.15
  338.2 1.8 convolution_bitcast_fusion.9
  340.0 12.1 %psum.60 = f32[64,64]{1,0:T(8,128)} all-reduce(f32[64,64]{1,0:T(8,128)} %convolution_bitcast_fusion.9), channel_id=1, replica_groups=mesh['group'=4,'bulk'=32] {'group'}, use_global_device_ids=true, to_apply=%region_10.14 | all-reduce | flops 4096 | bytes 32768 | tf_op jit(solution)/shard_map/psum | solution.py:26
  352.1 127.8 %psum.61 = f32[64,64]{1,0:T(8,128)} all-reduce(f32[64,64]{1,0:T(8,128)} %psum.60), channel_id=1, replica_groups=mesh['group'=4,'bulk'=32] {'bulk'}, use_global_device_ids=true, to_apply=%region_11.15 | all-reduce | flops 4096 | bytes 32768 | tf_op jit(solution)/shard_map/psum | solution.py:26
  479.9 1.4 copy.49
  484.6 1.4 bitcast_dynamic-update-slice_fusion.3
  486.0 1.4 bitcast_dynamic-update-slice_fusion.2
  488.0 5.7 collective-permute-start
  496.7 2.2 broadcast_select_fusion
  498.9 21.5 %collective-permute-done.1 = f32[221184]{0:T(1024)} collective-permute-done((f32[221184]{0:T(1024)}, f32[221184]{0:T(1024)}, u32[]{:S(2)}, u32[]{:S(2)}) %collective-permute-start.1) | collective-permute-done | bytes 884768 | tf_op jit(solution)/shard_map/ppermute | solution.py:13
  520.4 2.2 broadcast_select_fusion.1
  522.7 22.2 %collective-permute-done.2 = f32[221184]{0:T(1024)} collective-permute-done((f32[221184]{0:T(1024)}, f32[221184]{0:T(1024)}, u32[]{:S(2)}, u32[]{:S(2)}) %collective-permute-start.2) | collective-permute-done | bytes 884768 | tf_op jit(solution)/shard_map/ppermute | solution.py:13
  544.8 2.2 broadcast_select_fusion.2
  547.0 19.8 %collective-permute-done.3 = f32[221184]{0:T(1024)} collective-permute-done((f32[221184]{0:T(1024)}, f32[221184]{0:T(1024)}, u32[]{:S(2)}, u32[]{:S(2)}) %collective-permute-start.3) | collective-permute-done | bytes 884768 | tf_op jit(solution)/shard_map/ppermute | solution.py:13
  566.8 2.2 broadcast_select_fusion.3
  569.8 19.7 %collective-permute-done.4 = f32[221184]{0:T(1024)} collective-permute-done((f32[221184]{0:T(1024)}, f32[221184]{0:T(1024)}, u32[]{:S(2)}, u32[]{:S(2)}) %collective-permute-start.4) | collective-permute-done | bytes 884768 | tf_op jit(solution)/shard_map/ppermute | solution.py:13
  591.7 2.0 fusion.40
  596.6 1.4 and_reduce_fusion
  600.6 3.2 fusion
  603.8 2.5 broadcast.320
  606.3 7.8 scatter_fusion.1
  614.4 10.3 %all_gather.15 = f32[8,64,128]{2,1,0:T(8,128)} all-gather(f32[2,64,128]{2,1,0:T(8,128)S(1)} %slice.243), channel_id=1, replica_groups=mesh['group'=4,'bulk'=32] {'group'}, dimensions={0}, use_global_device_ids=true | all-gather | bytes 327680 | tf_op jit(solution)/shard_map/all_gather | solution.py:35
  624.7 2.1 fusion.35
  626.8 12.9 %all-gather.5.cloned.1.call-done = f32[128,64,128]{2,1,0:T(8,128)} async-done(((f32[4,64,128]{2,1,0:T(8,128)}), f32[128,64,128]{2,1,0:T(8,128)}) %all-gather.5.cloned.1.call-update) | async-done | bytes 4194320 | tf_op jit(solution)/shard_map/all_gather | solution.py:41
  639.7 4.0 gather_fusion.7
  643.7 5.4 fusion.15
  649.1 73.8 %reduce-scatter.5.cloned.1.call-done = f32[4,64,128]{2,1,0:T(8,128)} async-done(((f32[128,64,128]{2,1,0:T(8,128)}), f32[4,64,128]{2,1,0:T(8,128)}) %reduce-scatter.5.cloned.1.call-update) | async-done | bytes 131088 | tf_op jit(solution)/shard_map/reduce_scatter | solution.py:43
  723.0 1.7 fusion.19
  724.6 1.6 fusion.27
  726.5 13.2 %psum.62 = f32[64,64]{1,0:T(8,128)S(1)} all-reduce(f32[64,64]{1,0:T(8,128)S(1)} %convolution_bitcast_fusion.7), channel_id=1, replica_groups=mesh['group'=4,'bulk'=32] {'group'}, use_global_device_ids=true, to_apply=%region_16.20 | all-reduce | flops 4096 | bytes 32768 | tf_op jit(solution)/shard_map/psum | solution.py:26
  739.7 124.3 %psum.63 = f32[64,64]{1,0:T(8,128)S(1)} all-reduce(f32[64,64]{1,0:T(8,128)S(1)} %psum.62), channel_id=1, replica_groups=mesh['group'=4,'bulk'=32] {'bulk'}, use_global_device_ids=true, to_apply=%region_17.21 | all-reduce | flops 4096 | bytes 32768 | tf_op jit(solution)/shard_map/psum | solution.py:26
  864.2 5.8 cholesky.81
  871.4 4.9 custom-call.17
  (107 shorter events, 40.6 us)
Async XLA Ops:
  7.2 137.9 %copy-start = (f32[2,4,128,128]{3,2,1,0:T(8,128)S(1)}, f32[2,4,128,128]{3,2,1,0:T(8,128)}, u32[]{:S(2)}) copy-start(f32[2,4,128,128]{3,2,1,0:T(8,128)} %param.29) | copy-start | bytes 1572868
  7.2 18.1 %copy-start.3 = (f32[4,64,128]{2,1,0:T(8,128)S(1)}, f32[4,64,128]{2,1,0:T(8,128)}, u32[]{:S(2)}) copy-start(f32[4,64,128]{2,1,0:T(8,128)} %param.26) | copy-start | bytes 393220
  7.2 16.2 %copy-start.2 = (s32[512]{0:T(512)S(1)}, s32[512]{0:T(512)}, u32[]{:S(2)}) copy-start(s32[512]{0:T(512)} %param.31) | copy-start | bytes 6148
  7.2 4.3 copy-start.1
  7.2 55.2 %all-gather.3.cloned.1.call-start = ((), (), s32[]{:S(2)}) async-start(), calls=%async_computation.2 | async-start | bytes 4325376 | tf_op jit(solution)/shard_map/all_gather | solution.py:41
  7.3 1.9 copy-start.12
  9.9 133.5 %reduce-scatter.3.cloned.1.call-start = ((), (), s32[]{:S(2)}) async-start(), calls=%async_computation.3 | async-start | bytes 4325376 | tf_op jit(solution)/shard_map/reduce_scatter | solution.py:43
  39.0 600.7 %all-gather.5.cloned.1.call-start = ((), (), s32[]{:S(2)}) async-start(), calls=%async_computation.4 | async-start | bytes 4325376 | tf_op jit(solution)/shard_map/all_gather | solution.py:41
  71.8 421.8 %copy-start.14 = (s32[4]{0:T(128)S(1)}, s32[4]{0:T(128)}, u32[]{:S(2)}) copy-start(s32[4]{0:T(128)} %gather_fusion.3) | copy-start | bytes 52
  146.7 0.7 copy-start.8
  484.6 2.8 copy-start.4
  488.0 8.7 collective-permute-start
  498.9 21.5 %collective-permute-start.1 = (f32[221184]{0:T(1024)}, f32[221184]{0:T(1024)}, u32[]{:S(2)}, u32[]{:S(2)}) collective-permute-start(f32[221184]{0:T(1024)} %broadcast_select_fusion), channel_id=1, source_target_pairs={{0,2},{1,3},{2,0},{3,1},{4,6},{5,7},{6,4},{7,5},{8,10},{9,11},{10,... | collective-permute-start | bytes 2654216 | tf_op jit(solution)/shard_map/ppermute | solution.py:13
  522.6 46.4 %copy-start.15 = (s32[3]{0:T(128)S(1)}, s32[3]{0:T(128)}, u32[]{:S(2)}) copy-start(s32[3]{0:T(128)} %constant.237.clone.1) | copy-start | bytes 40
  522.6 47.2 %copy-start.9 = (f32[64,4,128]{2,0,1:T(8,128)S(1)}, f32[64,4,128]{2,0,1:T(8,128)}, u32[]{:S(2)}) copy-start(f32[64,4,128]{2,0,1:T(8,128)} %fusion.73) | copy-start | bytes 393220
  522.6 22.2 %collective-permute-start.2 = (f32[221184]{0:T(1024)}, f32[221184]{0:T(1024)}, u32[]{:S(2)}, u32[]{:S(2)}) collective-permute-start(f32[221184]{0:T(1024)} %broadcast_select_fusion.1), channel_id=1, source_target_pairs={{0,4},{1,5},{2,6},{3,7},{4,0},{5,1},{6,2},{7,3},{8,12},{9,13},{10,... | collective-permute-start | bytes 2654216 | tf_op jit(solution)/shard_map/ppermute | solution.py:13
  547.0 19.8 %collective-permute-start.3 = (f32[221184]{0:T(1024)}, f32[221184]{0:T(1024)}, u32[]{:S(2)}, u32[]{:S(2)}) collective-permute-start(f32[221184]{0:T(1024)} %broadcast_select_fusion.2), channel_id=1, source_target_pairs={{0,8},{1,9},{2,10},{3,11},{4,12},{5,13},{6,14},{7,15},{8,0},{9,1},... | collective-permute-start | bytes 2654216 | tf_op jit(solution)/shard_map/ppermute | solution.py:13
  547.0 48.7 %copy-start.13 = (s32[4,11,1]{1,0,2:T(4,128)S(1)}, s32[4,11,1]{1,0,2:T(4,128)}, u32[]{:S(2)}) copy-start(s32[4,11,1]{1,0,2:T(4,128)} %get-tuple-element.100) | copy-start | bytes 532
  569.0 20.5 %collective-permute-start.4 = (f32[221184]{0:T(1024)}, f32[221184]{0:T(1024)}, u32[]{:S(2)}, u32[]{:S(2)}) collective-permute-start(f32[221184]{0:T(1024)} %broadcast_select_fusion.3), channel_id=1, source_target_pairs={{0,16},{1,17},{2,18},{3,19},{4,20},{5,21},{6,22},{7,23},{8,24},{9,... | collective-permute-start | bytes 2654216 | tf_op jit(solution)/shard_map/ppermute | solution.py:13
  590.8 0.9 copy-start.7
  593.7 0.7 copy-start.10
  594.4 128.6 %reduce-scatter.5.cloned.1.call-start = ((), (), s32[]{:S(2)}) async-start(), calls=%async_computation.5 | async-start | bytes 4325376 | tf_op jit(solution)/shard_map/reduce_scatter | solution.py:43
  595.7 4.9 copy-start.5
  649.1 228.4 %copy-start.6 = (f32[4,64,128]{2,1,0:T(8,128)S(1)}, f32[4,64,128]{2,1,0:T(8,128)}, u32[]{:S(2)}) copy-start(f32[4,64,128]{2,1,0:T(8,128)} %get-tuple-element.97) | copy-start | bytes 393220
  649.1 229.3 %copy-start.11 = (f32[4,64,128]{2,1,0:T(8,128)S(1)}, f32[4,64,128]{2,1,0:T(8,128)}, u32[]{:S(2)}) copy-start(f32[4,64,128]{2,1,0:T(8,128)} %copy-done.10) | copy-start | bytes 393220
Sparse Core Ops, SparseCore 0:
  10.3 49.7 all-gather.2
  63.7 79.6 reduce-scatter.2
  594.5 45.1 all-gather.4
  643.2 79.7 reduce-scatter.4
